TPU v7x, 128 devices: a whole 4x4x4 slice. The times are simulated.
128 devices in a mesh: row: 16 (over y, x), col: 8 (over z, core).
Axes of the slice: x: 4, y: 4, z: 4, core: 2. Of those that a mesh axis runs over, the one named last changes fastest.
Arguments:
- layer_input: bfloat16 [768, 8192], P('col', 'row'), may hold values from -6 to 6
- out_grad: bfloat16 [768, 8192], P('col', 'row'), may hold values from -6 to 6
- gate_weight: bfloat16 [8192, 28672], P('row', 'col'), may hold values from -0.0625 to 0.0625
- up_weight: bfloat16 [8192, 28672], P('row', 'col'), may hold values from -0.0625 to 0.0625
- down_weight: bfloat16 [28672, 8192], P('col', 'row'), may hold values from -0.03125 to 0.03125
Outputs:
- input_grad: bfloat16 [768, 8192], P('col', 'row')
- gate_grad: bfloat16 [8192, 28672], P('row', 'col')
- up_grad: bfloat16 [8192, 28672], P('row', 'col')
- down_grad: bfloat16 [28672, 8192], P('col', 'row')
All inputs are finite; a program needn't handle non-finite values.
Results may differ from a plain program's by a relative error of at most 0.033.
Values may be sent and summed in bfloat16 or wider, within the bound.
A program may use at most 192 MiB of HBM per device.

v0:
```python
import jax
import jax.numpy as jnp
from jax import lax
from jax.sharding import PartitionSpec as P


def swiglu_back(summed, width):
    gate = summed[:, :width]
    up = summed[:, width : 2 * width]
    hidden_grad = summed[:, 2 * width :]
    sigma = jax.nn.sigmoid(gate)
    swish = gate * sigma
    hidden = (swish * up).astype(jnp.bfloat16)
    up_delta = (hidden_grad * swish).astype(jnp.bfloat16)
    gate_delta = (hidden_grad * up * sigma * (1.0 + gate * (1.0 - sigma))).astype(jnp.bfloat16)
    return (hidden, gate_delta, up_delta)


def local(layer_input, out_grad, gate_weight, up_weight, down_weight):
    input_rows, cot_rows = (
        lax.all_gather(layer_input, "col", axis=0, tiled=True),
        lax.all_gather(out_grad, "col", axis=0, tiled=True),
    )
    tokens = input_rows.shape[0]
    width = gate_weight.shape[1]
    both_weights = jnp.concatenate([gate_weight, up_weight], axis=1)
    contract_last = (((1,), (1,)), ((), ()))
    contract_first = (((0,), (0,)), ((), ()))
    left = input_rows
    right = cot_rows
    gate_up = jnp.dot(left, both_weights, preferred_element_type=jnp.float32)
    hidden_grad = lax.dot_general(
        right, down_weight, contract_last, preferred_element_type=jnp.float32
    )
    summed = lax.psum_scatter(
        jnp.concatenate([gate_up, hidden_grad], axis=1).astype(jnp.bfloat16),
        "row",
        scatter_dimension=0,
        tiled=True,
    ).astype(jnp.float32)
    hidden, gate_delta, up_delta = swiglu_back(summed, width)
    accumulate_hidden = lax.all_gather(hidden, "row", axis=0, tiled=True)
    accumulate_gate_delta = lax.all_gather(gate_delta, "row", axis=0, tiled=True)
    accumulate_up_delta = lax.all_gather(up_delta, "row", axis=0, tiled=True)
    left = input_rows
    right = cot_rows
    down_sum = lax.dot_general(
        accumulate_hidden, right, contract_first, preferred_element_type=jnp.float32
    )
    gate_sum = lax.dot_general(
        left, accumulate_gate_delta, contract_first, preferred_element_type=jnp.float32
    )
    up_sum = lax.dot_general(
        left, accumulate_up_delta, contract_first, preferred_element_type=jnp.float32
    )
    term = lax.dot_general(
        accumulate_gate_delta, gate_weight, contract_last, preferred_element_type=jnp.float32
    )
    term = term + lax.dot_general(
        accumulate_up_delta, up_weight, contract_last, preferred_element_type=jnp.float32
    )
    factor = 1.0 / tokens**0.5
    down_grad = (down_sum * factor).astype(jnp.bfloat16)
    gate_grad = (gate_sum * factor).astype(jnp.bfloat16)
    up_grad = (up_sum * factor).astype(jnp.bfloat16)
    input_grad = lax.psum_scatter(term.astype(jnp.bfloat16), "col", scatter_dimension=0, tiled=True)
    return (input_grad, gate_grad, up_grad, down_grad)


def solution(mesh):
    placed = (P("col", "row"), P("col", "row"), P("row", "col"), P("row", "col"), P("col", "row"))
    return jax.shard_map(
        local,
        mesh=mesh,
        in_specs=placed,
        out_specs=(P("col", "row"), P("row", "col"), P("row", "col"), P("col", "row")),
        check_vma=False,
    )
```

profile of v0, /device:TPU:0, one launch (start us, length us, event | category | flops | bytes accessed | tf_op | source)
XLA Modules:
  0.0 429.2 jit_solution(3540597175312089114)
XLA Ops:
  7.2 0.0 reduce-scatter.7.cloned.1.call-start
  7.2 14.9 %all_gather.15 = bf16[768,512]{1,0:T(8,128)(2,1)S(1)} all-gather(bf16[96,512]{1,0:T(8,128)(2,1)} %param.5), channel_id=1, replica_groups=mesh['row'=16,'col'=8] {'col'}, dimensions={0}, use_global_device_ids=true | all-gather | bytes 884736 | tf_op jit(solution)/shard_map/all_gather | solution.py:21
  22.1 13.6 %all_gather.16 = bf16[768,512]{1,0:T(8,128)(2,1)S(1)} all-gather(bf16[96,512]{1,0:T(8,128)(2,1)} %param.6), channel_id=1, replica_groups=mesh['row'=16,'col'=8] {'col'}, dimensions={0}, use_global_device_ids=true | all-gather | bytes 884736 | tf_op jit(solution)/shard_map/all_gather | solution.py:22
  35.7 7.5 %convolution_convert_fusion.1 = bf16[768,3584]{0,1:T(8,128)(2,1)} fusion(bf16[768,512]{1,0:T(8,128)(2,1)S(1)} %all_gather.16, bf16[3584,512]{1,0:T(8,128)(2,1)} %param.9), kind=kOutput, calls=%fused_computation.9 | convolution fusion | flops 2821324800 | bytes 9961472 | tf_op jit(solution)/shard_map/dot_general | solution.py:32
  43.2 13.8 %fusion = bf16[768,7168]{0,1:T(8,128)(2,1)} fusion(bf16[768,512]{1,0:T(8,128)(2,1)S(1)} %all_gather.15, bf16[512,3584]{1,0:T(8,128)(2,1)} %param.8, bf16[512,3584]{1,0:T(8,128)(2,1)} %param.7), kind=kOutput, calls=%fused_computation.2 | convolution fusion | flops 5657329664 | bytes 19136512 | tf_op jit(solution)/shard_map/dot_general | solution.py:31
  57.0 18.5 %pad_maximum_fusion = bf16[768,10752]{0,1:T(8,128)(2,1)} fusion(bf16[768,3584]{0,1:T(8,128)(2,1)} %convolution_convert_fusion.1, bf16[768,7168]{0,1:T(8,128)(2,1)} %fusion), kind=kLoop, calls=%fused_computation | loop fusion | flops 33030144 | bytes 33030144 | tf_op jit(solution)/shard_map/concatenate | solution.py:36
  75.5 22.3 %copy.23 = bf16[768,10752]{1,0:T(8,128)(2,1)} copy(bf16[768,10752]{0,1:T(8,128)(2,1)} %pad_maximum_fusion) | data formatting | bytes 33030144
  97.8 0.0 reduce-scatter.7.cloned.1.call-update
  97.8 0.0 all-gather.4.cloned.1.call-start
  97.9 110.7 %reduce-scatter.7.cloned.1.call-done = bf16[48,10752]{1,0:T(8,128)(2,1)} async-done(((bf16[768,10752]{1,0:T(8,128)(2,1)}), bf16[48,10752]{1,0:T(8,128)(2,1)}) %reduce-scatter.7.cloned.1.call-update) | async-done | bytes 1032208 | tf_op jit(solution)/shard_map/reduce_scatter | solution.py:35
  208.6 1.4 convert_element_type.31
  210.0 1.3 multiply_convert_fusion.3
  211.3 0.0 all-gather.4.cloned.1.call-update
  211.3 0.0 all-gather.6.cloned.1.call-start
  211.3 0.7 all-gather.6.cloned.1.call-update
  212.0 0.0 all-gather.8.cloned.1.call-start
  212.1 0.5 all-gather.8.cloned.1.call-update
  212.6 0.2 reduce-scatter.5.cloned.1.call-start
  212.8 55.8 %all-gather.4.cloned.1.call-done = bf16[768,3584]{1,0:T(8,128)(2,1)} async-done(((bf16[48,3584]{1,0:T(8,128)(2,1)}), bf16[768,3584]{1,0:T(8,128)(2,1)}) %all-gather.4.cloned.1.call-update) | async-done | bytes 5505040 | tf_op jit(solution)/shard_map/all_gather | solution.py:43
  268.6 6.1 %fusion.8 = f32[768,512]{1,0:T(8,128)S(1)} fusion(bf16[768,3584]{1,0:T(8,128)(2,1)} %all-gather.4.cloned.1.call-done, bf16[512,3584]{1,0:T(8,128)(2,1)} %param.7), kind=kOutput, calls=%fused_computation.19 | convolution fusion | flops 2818572288 | bytes 10747904 | tf_op jit(solution)/shard_map/dot_general | solution.py:56
  274.8 54.1 %all-gather.6.cloned.1.call-done = bf16[768,3584]{1,0:T(8,128)(2,1)} async-done(((bf16[48,3584]{1,0:T(8,128)(2,1)}), bf16[768,3584]{1,0:T(8,128)(2,1)}) %all-gather.6.cloned.1.call-update) | async-done | bytes 5505040 | tf_op jit(solution)/shard_map/all_gather | solution.py:44
  328.8 7.6 %add_convert_fusion = bf16[768,512]{1,0:T(8,128)(2,1)} fusion(f32[768,512]{1,0:T(8,128)S(1)} %fusion.8, bf16[768,3584]{1,0:T(8,128)(2,1)} %all-gather.6.cloned.1.call-done, bf16[512,3584]{1,0:T(8,128)(2,1)} %param.8), kind=kOutput, calls=%fused_computation.12 | convolution fusion | flops 2819358720 | bytes 11534336 | tf_op jit(solution)/shard_map/dot_general | solution.py:59
  336.4 0.0 reduce-scatter.5.cloned.1.call-update
  336.5 7.1 %fusion.5 = bf16[512,3584]{0,1:T(8,128)(2,1)} fusion(bf16[768,3584]{1,0:T(8,128)(2,1)} %all-gather.6.cloned.1.call-done, bf16[768,512]{1,0:T(8,128)(2,1)S(1)} %all_gather.15), kind=kOutput, calls=%fused_computation.11 | convolution fusion | flops 2822242304 | bytes 9961472 | tf_op jit(solution)/shard_map/dot_general | solution.py:53
  343.6 5.9 %copy.21 = bf16[512,3584]{1,0:T(8,128)(2,1)} copy(bf16[512,3584]{0,1:T(8,128)(2,1)} %fusion.5) | data formatting | bytes 7340032
  349.5 7.1 %fusion.4 = bf16[512,3584]{0,1:T(8,128)(2,1)} fusion(bf16[768,3584]{1,0:T(8,128)(2,1)} %all-gather.4.cloned.1.call-done, bf16[768,512]{1,0:T(8,128)(2,1)S(1)} %all_gather.15), kind=kOutput, calls=%fused_computation.10 | convolution fusion | flops 2822242304 | bytes 9961472 | tf_op jit(solution)/shard_map/dot_general | solution.py:50
  356.6 5.9 %copy.20 = bf16[512,3584]{1,0:T(8,128)(2,1)} copy(bf16[512,3584]{0,1:T(8,128)(2,1)} %fusion.4) | data formatting | bytes 7340032
  362.5 25.8 %all-gather.8.cloned.1.call-done = bf16[768,3584]{1,0:T(8,128)(2,1)} async-done(((bf16[48,3584]{1,0:T(8,128)(2,1)}), bf16[768,3584]{1,0:T(8,128)(2,1)}) %all-gather.8.cloned.1.call-update) | async-done | bytes 5505040 | tf_op jit(solution)/shard_map/all_gather | solution.py:42
  388.3 7.1 %multiply_convert_fusion = bf16[3584,512]{1,0:T(8,128)(2,1)} fusion(bf16[768,3584]{1,0:T(8,128)(2,1)} %all-gather.8.cloned.1.call-done, bf16[768,512]{1,0:T(8,128)(2,1)S(1)} %all_gather.16), kind=kOutput, calls=%fused_computation.6 | convolution fusion | flops 2822242304 | bytes 9961472 | tf_op jit(solution)/shard_map/dot_general | solution.py:47
  395.4 27.2 %reduce-scatter.5.cloned.1.call-done = bf16[96,512]{1,0:T(8,128)(2,1)} async-done(((bf16[768,512]{1,0:T(8,128)(2,1)}), bf16[96,512]{1,0:T(8,128)(2,1)}) %reduce-scatter.5.cloned.1.call-update) | async-done | bytes 98320 | tf_op jit(solution)/shard_map/reduce_scatter | solution.py:66
Async XLA Ops:
  7.2 201.5 %reduce-scatter.7.cloned.1.call-start = ((), (), s32[]{:S(2)}) async-start(), calls=%async_computation.6 | async-start | bytes 17547264 | tf_op jit(solution)/shard_map/reduce_scatter | solution.py:35
  97.8 170.8 %all-gather.4.cloned.1.call-start = ((), (), s32[]{:S(2)}) async-start(), calls=%async_computation.2 | async-start | bytes 5849088 | tf_op jit(solution)/shard_map/all_gather | solution.py:43
  211.3 117.5 %all-gather.6.cloned.1.call-start = ((), (), s32[]{:S(2)}) async-start(), calls=%async_computation.3 | async-start | bytes 5849088 | tf_op jit(solution)/shard_map/all_gather | solution.py:44
  212.0 176.3 %all-gather.8.cloned.1.call-start = ((), (), s32[]{:S(2)}) async-start(), calls=%async_computation.5 | async-start | bytes 5849088 | tf_op jit(solution)/shard_map/all_gather | solution.py:42
  212.6 210.0 %reduce-scatter.5.cloned.1.call-start = ((), (), s32[]{:S(2)}) async-start(), calls=%async_computation.4 | async-start | bytes 884736 | tf_op jit(solution)/shard_map/reduce_scatter | solution.py:66
Sparse Core Ops, SparseCore 0:
  98.0 110.6 reduce-scatter.6
  211.6 57.0 all-gather.3
  271.6 57.2 all-gather.5
  331.1 57.2 all-gather.7
  391.3 31.3 reduce-scatter.4
where the time goes:
time: 430 us; the launch traced here: 429 us
  waiting for transfers between devices  275 us (64%)
  matrix products  56.3 us (13%)
  local copies, waits for them, and re-layouts  34.2 us (8%)
  blocking collectives  28.5 us (7%)
  other arithmetic  21.2 us (5%)
  between operations  13.8 us (3%)
    reduce_scatter x1, waiting for transfers between devices, local(): lax.psum_scatter(jnp.concatenate([gate_up, hidden_grad], axis=1).astype(j...  111 us
    all_gather x1, waiting for transfers between devices, local(): lax.all_gather(gate_delta, 'row', axis=0, tiled=True)  55.8 us
    all_gather x1, waiting for transfers between devices, local(): accumulate_up_delta = lax.all_gather(up_delta, 'row', axis=0, tiled=True)  54.1 us
    unnamed x3, local copies, waits for them, and re-layouts  34.2 us
    reduce_scatter x1, waiting for transfers between devices, local(): lax.psum_scatter(term.astype(jnp.bfloat16), 'col', scatter_dimension=0, t...  27.2 us
    all_gather x1, waiting for transfers between devices, local(): accumulate_hidden = lax.all_gather(hidden, 'row', axis=0, tiled=True)  25.8 us
    concatenate x1, other arithmetic, local(): jnp.concatenate([gate_up, hidden_grad], axis=1).astype(jnp.bfloat16)  18.5 us
    all_gather x1, blocking collectives, local(): lax.all_gather(layer_input, 'col', axis=0, tiled=True)  14.9 us
  transfers between devices with their start and end apart: 5, of which 5 were waited for; matrix products, arithmetic and copies ran while one was open for 11% of the time, Pallas kernels for 0%

commit v1 on v0

--- a/solution.py
+++ b/solution.py
@@ -2,6 +2,12 @@
 import jax.numpy as jnp
 from jax import lax
 from jax.sharding import PartitionSpec as P
+
+
+def joined_along(parts, dim):
+    lengths = list(parts.shape[1:])
+    lengths[dim] *= parts.shape[0]
+    return jnp.moveaxis(parts, 0, dim).reshape(lengths)
 
 
 def swiglu_back(summed, width):
@@ -39,7 +45,19 @@
         tiled=True,
     ).astype(jnp.float32)
     hidden, gate_delta, up_delta = swiglu_back(summed, width)
-    accumulate_hidden = lax.all_gather(hidden, "row", axis=0, tiled=True)
+    peers = lax.axis_size("row")
+    pairs = [(i, (i + 1) % peers) for i in range(peers)]
+    back = [(b, a) for a, b in pairs]
+    lower, upper = ([], [])
+    for step in range(peers - 1):
+        if step % 2 == 0:
+            lower.append(lax.ppermute(lower[-1] if lower else hidden, "row", pairs))
+        else:
+            upper.append(lax.ppermute(upper[-1] if upper else hidden, "row", back))
+    blocks = jnp.stack([*lower[::-1], hidden, *upper])
+    shift = lax.axis_index("row") - len(lower)
+    blocks = blocks[(jnp.arange(peers) - shift) % peers]
+    accumulate_hidden = joined_along(blocks, 0)
     accumulate_gate_delta = lax.all_gather(gate_delta, "row", axis=0, tiled=True)
     accumulate_up_delta = lax.all_gather(up_delta, "row", axis=0, tiled=True)
     left = input_rows

time: 430 us -> 422 us (0.981)
  waiting for transfers between devices: 275 us -> 198 us
  starting transfers between devices: 0.38 us -> 40.7 us
  local copies, waits for them, and re-layouts: 34.2 us -> 60.9 us
    ppermute x0 -> x15, waiting for transfers between devices: none -> 71 us  [the longest x8 59.8 us: local(): lower.append(lax.ppermute(lower[-1] if lower else hidden, 'row', pairs))]
    all_gather x1, waiting for transfers between devices: 55.8 us -> 0.01 us  [local(): lax.all_gather(gate_delta, 'row', axis=0, tiled=True)]
    ppermute x0 -> x15, starting transfers between devices: none -> 40.5 us  [the longest x7 39.2 us: local(): upper.append(lax.ppermute(upper[-1] if upper else hidden, 'row', back))]
    all_gather x1, waiting for transfers between devices: 54.1 us -> 15.9 us  [local(): accumulate_up_delta = lax.all_gather(up_delta, 'row', axis=0, tiled=True)]
    reduce_scatter x1, waiting for transfers between devices: 27.2 us -> 0.01 us  [local(): lax.psum_scatter(term.astype(jnp.bfloat16), 'col', scatter_dimension=0, t...]
    all_gather x1 -> x0, waiting for transfers between devices: 25.8 us -> none  [local(): accumulate_hidden = lax.all_gather(hidden, 'row', axis=0, tiled=True)]
    unnamed x3 -> x34, local copies, waits for them, and re-layouts: 34.2 us -> 54.2 us
    gather x0 -> x1, local copies, waits for them, and re-layouts: none -> 5.95 us  [local(): blocks = blocks[(jnp.arange(peers) - shift) % peers]]
  transfers between devices with their start and end apart: 5 -> 19, of which waited for: 5 -> 12; matrix products, arithmetic and copies ran while one was open for 11% -> 16% of each run, Pallas kernels for 0% -> 0%
where the time goes in v1:
time: 422 us; the launch traced here: 419 us
  waiting for transfers between devices  198 us (47%)
  local copies, waits for them, and re-layouts  60.9 us (14%)
  matrix products  56.5 us (13%)
  starting transfers between devices  40.7 us (10%)
  blocking collectives  28.5 us (7%)
  other arithmetic  21.1 us (5%)
  between operations  13.9 us (3%)
    reduce_scatter x1, waiting for transfers between devices, local(): lax.psum_scatter(jnp.concatenate([gate_up, hidden_grad], axis=1).astype(j...  111 us
    ppermute x8, waiting for transfers between devices, local(): lower.append(lax.ppermute(lower[-1] if lower else hidden, 'row', pairs))  59.8 us
    unnamed x34, local copies, waits for them, and re-layouts  54.2 us
    ppermute x7, starting transfers between devices, local(): upper.append(lax.ppermute(upper[-1] if upper else hidden, 'row', back))  39.2 us
    concatenate x1, other arithmetic, local(): jnp.concatenate([gate_up, hidden_grad], axis=1).astype(jnp.bfloat16)  18.5 us
    all_gather x1, waiting for transfers between devices, local(): accumulate_up_delta = lax.all_gather(up_delta, 'row', axis=0, tiled=True)  15.9 us
    all_gather x1, blocking collectives, local(): lax.all_gather(layer_input, 'col', axis=0, tiled=True)  14.9 us
    dot_general x1, matrix products, local(): gate_up = jnp.dot(left, both_weights, preferred_element_type=jnp.float32)  13.8 us
  transfers between devices with their start and end apart: 19, of which 12 were waited for; matrix products, arithmetic and copies ran while one was open for 16% of the time, Pallas kernels for 0%

profile of v1, /device:TPU:0, one launch (start us, length us, event | category | flops | bytes accessed | tf_op | source)
XLA Modules:
  0.0 419.2 jit_solution(1843405410841983455)
XLA Ops:
  7.2 14.9 %all_gather.12 = bf16[768,512]{1,0:T(8,128)(2,1)S(1)} all-gather(bf16[96,512]{1,0:T(8,128)(2,1)} %param.5), channel_id=1, replica_groups=mesh['row'=16,'col'=8] {'col'}, dimensions={0}, use_global_device_ids=true | all-gather | bytes 884736 | tf_op jit(solution)/shard_map/all_gather | solution.py:27
  22.1 13.6 %all_gather.13 = bf16[768,512]{1,0:T(8,128)(2,1)S(1)} all-gather(bf16[96,512]{1,0:T(8,128)(2,1)} %param.6), channel_id=1, replica_groups=mesh['row'=16,'col'=8] {'col'}, dimensions={0}, use_global_device_ids=true | all-gather | bytes 884736 | tf_op jit(solution)/shard_map/all_gather | solution.py:28
  35.7 7.4 %convolution_convert_fusion.1 = bf16[768,3584]{0,1:T(8,128)(2,1)} fusion(bf16[768,512]{1,0:T(8,128)(2,1)S(1)} %all_gather.13, bf16[3584,512]{1,0:T(8,128)(2,1)} %param.9), kind=kOutput, calls=%fused_computation.10 | convolution fusion | flops 2821324800 | bytes 9961472 | tf_op jit(solution)/shard_map/dot_general | solution.py:38
  43.2 13.8 %fusion = bf16[768,7168]{0,1:T(8,128)(2,1)} fusion(bf16[768,512]{1,0:T(8,128)(2,1)S(1)} %all_gather.12, bf16[512,3584]{1,0:T(8,128)(2,1)} %param.8, bf16[512,3584]{1,0:T(8,128)(2,1)} %param.7), kind=kOutput, calls=%fused_computation.3 | convolution fusion | flops 5657329664 | bytes 19136512 | tf_op jit(solution)/shard_map/dot_general | solution.py:37
  57.0 18.5 %pad_maximum_fusion = bf16[768,10752]{0,1:T(8,128)(2,1)} fusion(bf16[768,3584]{0,1:T(8,128)(2,1)} %convolution_convert_fusion.1, bf16[768,7168]{0,1:T(8,128)(2,1)} %fusion), kind=kLoop, calls=%fused_computation.1 | loop fusion | flops 33030144 | bytes 33030144 | tf_op jit(solution)/shard_map/concatenate | solution.py:42
  75.4 22.3 %copy.29 = bf16[768,10752]{1,0:T(8,128)(2,1)} copy(bf16[768,10752]{0,1:T(8,128)(2,1)} %pad_maximum_fusion) | data formatting | bytes 33030144
  97.9 110.7 %reduce-scatter.7.cloned.1.call-done = bf16[48,10752]{1,0:T(8,128)(2,1)} async-done(((bf16[768,10752]{1,0:T(8,128)(2,1)}), bf16[48,10752]{1,0:T(8,128)(2,1)}) %reduce-scatter.7.cloned.1.call-update) | async-done | bytes 1032208 | tf_op jit(solution)/shard_map/reduce_scatter | solution.py:41
  212.4 11.6 %collective-permute-done = bf16[48,3584]{1,0:T(8,128)(2,1)S(1)} collective-permute-done((bf16[48,3584]{1,0:T(8,128)(2,1)S(1)}, bf16[48,3584]{1,0:T(8,128)(2,1)S(1)}, u32[]{:S(2)}, u32[]{:S(2)}) %collective-permute-start) | collective-permute-done | bytes 344096 | tf_op jit(solution)/shard_map/ppermute | solution.py:54
  224.0 5.3 %collective-permute-start.8 = (bf16[48,3584]{1,0:T(8,128)(2,1)S(1)}, bf16[48,3584]{1,0:T(8,128)(2,1)S(1)}, u32[]{:S(2)}, u32[]{:S(2)}) collective-permute-start(bf16[48,3584]{1,0:T(8,128)(2,1)S(1)} %get-tuple-element.20), channel_id=1, source_target_pairs={{8,0},{16,8},{24,16},{32,24},{40,32},{48,40},{56,48},{64,56},{72,6... | collective-permute-start | bytes 1032200 | tf_op jit(solution)/shard_map/ppermute | solution.py:56
  229.4 10.7 %collective-permute-done.1 = bf16[48,3584]{1,0:T(8,128)(2,1)S(1)} collective-permute-done((bf16[48,3584]{1,0:T(8,128)(2,1)S(1)}, bf16[48,3584]{1,0:T(8,128)(2,1)S(1)}, u32[]{:S(2)}, u32[]{:S(2)}) %collective-permute-start.1) | collective-permute-done | bytes 344096 | tf_op jit(solution)/shard_map/ppermute | solution.py:54
  240.0 5.3 %collective-permute-start.9 = (bf16[48,3584]{1,0:T(8,128)(2,1)S(1)}, bf16[48,3584]{1,0:T(8,128)(2,1)S(1)}, u32[]{:S(2)}, u32[]{:S(2)}) collective-permute-start(bf16[48,3584]{1,0:T(8,128)(2,1)S(1)} %collective-permute-done.8), channel_id=1, source_target_pairs={{8,0},{16,8},{24,16},{32,24},{40,32},{48,40},{56,48},{64,56},{72,6... | collective-permute-start | bytes 1032200 | tf_op jit(solution)/shard_map/ppermute | solution.py:56
  245.4 6.6 %collective-permute-done.2 = bf16[48,3584]{1,0:T(8,128)(2,1)S(1)} collective-permute-done((bf16[48,3584]{1,0:T(8,128)(2,1)S(1)}, bf16[48,3584]{1,0:T(8,128)(2,1)S(1)}, u32[]{:S(2)}, u32[]{:S(2)}) %collective-permute-start.2) | collective-permute-done | bytes 344096 | tf_op jit(solution)/shard_map/ppermute | solution.py:54
  252.0 6.2 %collective-permute-done.9 = bf16[48,3584]{1,0:T(8,128)(2,1)S(1)} collective-permute-done((bf16[48,3584]{1,0:T(8,128)(2,1)S(1)}, bf16[48,3584]{1,0:T(8,128)(2,1)S(1)}, u32[]{:S(2)}, u32[]{:S(2)}) %collective-permute-start.9) | collective-permute-done | bytes 344096 | tf_op jit(solution)/shard_map/ppermute | solution.py:56
  258.1 5.8 %collective-permute-start.10 = (bf16[48,3584]{1,0:T(8,128)(2,1)S(1)}, bf16[48,3584]{1,0:T(8,128)(2,1)S(1)}, u32[]{:S(2)}, u32[]{:S(2)}) collective-permute-start(bf16[48,3584]{1,0:T(8,128)(2,1)S(1)} %collective-permute-done.9), channel_id=1, source_target_pairs={{8,0},{16,8},{24,16},{32,24},{40,32},{48,40},{56,48},{64,56},{72,6... | collective-permute-start | bytes 1032200 | tf_op jit(solution)/shard_map/ppermute | solution.py:56
  263.9 8.5 %collective-permute-done.3 = bf16[48,3584]{1,0:T(8,128)(2,1)S(1)} collective-permute-done((bf16[48,3584]{1,0:T(8,128)(2,1)S(1)}, bf16[48,3584]{1,0:T(8,128)(2,1)S(1)}, u32[]{:S(2)}, u32[]{:S(2)}) %collective-permute-start.3) | collective-permute-done | bytes 344096 | tf_op jit(solution)/shard_map/ppermute | solution.py:54
  272.4 5.0 %collective-permute-done.10 = bf16[48,3584]{1,0:T(8,128)(2,1)S(1)} collective-permute-done((bf16[48,3584]{1,0:T(8,128)(2,1)S(1)}, bf16[48,3584]{1,0:T(8,128)(2,1)S(1)}, u32[]{:S(2)}, u32[]{:S(2)}) %collective-permute-start.10) | collective-permute-done | bytes 344096 | tf_op jit(solution)/shard_map/ppermute | solution.py:56
  277.5 5.8 %collective-permute-start.11 = (bf16[48,3584]{1,0:T(8,128)(2,1)S(1)}, bf16[48,3584]{1,0:T(8,128)(2,1)S(1)}, u32[]{:S(2)}, u32[]{:S(2)}) collective-permute-start(bf16[48,3584]{1,0:T(8,128)(2,1)S(1)} %collective-permute-done.10), channel_id=1, source_target_pairs={{8,0},{16,8},{24,16},{32,24},{40,32},{48,40},{56,48},{64,56},{72,6... | collective-permute-start | bytes 1032200 | tf_op jit(solution)/shard_map/ppermute | solution.py:56
  283.3 6.7 %collective-permute-done.4 = bf16[48,3584]{1,0:T(8,128)(2,1)S(1)} collective-permute-done((bf16[48,3584]{1,0:T(8,128)(2,1)S(1)}, bf16[48,3584]{1,0:T(8,128)(2,1)S(1)}, u32[]{:S(2)}, u32[]{:S(2)}) %collective-permute-start.4) | collective-permute-done | bytes 344096 | tf_op jit(solution)/shard_map/ppermute | solution.py:54
  290.8 5.3 %collective-permute-start.12 = (bf16[48,3584]{1,0:T(8,128)(2,1)S(1)}, bf16[48,3584]{1,0:T(8,128)(2,1)}, u32[]{:S(2)}, u32[]{:S(2)}) collective-permute-start(bf16[48,3584]{1,0:T(8,128)(2,1)S(1)} %collective-permute-done.11), channel_id=1, source_target_pairs={{8,0},{16,8},{24,16},{32,24},{40,32},{48,40},{56,48},{64,56},{72,6... | collective-permute-start | bytes 1032200 | tf_op jit(solution)/shard_map/ppermute | solution.py:56
  296.1 5.7 %collective-permute-done.5 = bf16[48,3584]{1,0:T(8,128)(2,1)S(1)} collective-permute-done((bf16[48,3584]{1,0:T(8,128)(2,1)S(1)}, bf16[48,3584]{1,0:T(8,128)(2,1)S(1)}, u32[]{:S(2)}, u32[]{:S(2)}) %collective-permute-start.5) | collective-permute-done | bytes 344096 | tf_op jit(solution)/shard_map/ppermute | solution.py:54
  301.8 5.9 %collective-permute-start.13 = (bf16[48,3584]{1,0:T(8,128)(2,1)}, bf16[48,3584]{1,0:T(8,128)(2,1)}, u32[]{:S(2)}, u32[]{:S(2)}) collective-permute-start(bf16[48,3584]{1,0:T(8,128)(2,1)} %collective-permute-done.12), channel_id=1, source_target_pairs={{8,0},{16,8},{24,16},{32,24},{40,32},{48,40},{56,48},{64,56},{72,6... | collective-permute-start | bytes 1032200 | tf_op jit(solution)/shard_map/ppermute | solution.py:56
  312.9 5.7 %collective-permute-start.14 = (bf16[48,3584]{1,0:T(8,128)(2,1)}, bf16[48,3584]{1,0:T(8,128)(2,1)S(1)}, u32[]{:S(2)}, u32[]{:S(2)}) collective-permute-start(bf16[48,3584]{1,0:T(8,128)(2,1)} %collective-permute-done.13), channel_id=1, source_target_pairs={{8,0},{16,8},{24,16},{32,24},{40,32},{48,40},{56,48},{64,56},{72,6... | collective-permute-start | bytes 1032200 | tf_op jit(solution)/shard_map/ppermute | solution.py:56
  318.6 5.0 %collective-permute-done.7 = bf16[48,3584]{1,0:T(8,128)(2,1)} collective-permute-done((bf16[48,3584]{1,0:T(8,128)(2,1)}, bf16[48,3584]{1,0:T(8,128)(2,1)}, u32[]{:S(2)}, u32[]{:S(2)}) %collective-permute-start.7) | collective-permute-done | bytes 344096 | tf_op jit(solution)/shard_map/ppermute | solution.py:54
  343.7 6.0 %gather_fusion = bf16[16,48,3584]{2,1,0:T(8,128)(2,1)} fusion(bf16[16,48,3584]{2,1,0:T(8,128)(2,1)} %bitcast_dynamic-update-slice_fusion, s32[1024]{0:T(1024)S(1)} %pad_clamp_fusion), kind=kCustom, calls=%fused_computation | custom fusion | bytes 11010112 | tf_op jit(solution)/shard_map/gather | solution.py:59
  349.6 6.1 %fusion.10 = f32[768,512]{1,0:T(8,128)S(1)} fusion(bf16[768,3584]{1,0:T(8,128)(2,1)} %all-gather.3.cloned.1.call-done, bf16[512,3584]{1,0:T(8,128)(2,1)} %param.7), kind=kOutput, calls=%fused_computation.43 | convolution fusion | flops 2818572288 | bytes 10747904 | tf_op jit(solution)/shard_map/dot_general | solution.py:74
  355.7 15.9 %all-gather.5.cloned.1.call-done = bf16[768,3584]{1,0:T(8,128)(2,1)} async-done(((bf16[48,3584]{1,0:T(8,128)(2,1)}), bf16[768,3584]{1,0:T(8,128)(2,1)}) %all-gather.5.cloned.1.call-update) | async-done | bytes 5505040 | tf_op jit(solution)/shard_map/all_gather | solution.py:62
  371.6 7.6 %add_convert_fusion = bf16[768,512]{1,0:T(8,128)(2,1)} fusion(f32[768,512]{1,0:T(8,128)S(1)} %fusion.10, bf16[768,3584]{1,0:T(8,128)(2,1)} %all-gather.5.cloned.1.call-done, bf16[512,3584]{1,0:T(8,128)(2,1)} %param.8), kind=kOutput, calls=%fused_computation.13 | convolution fusion | flops 2819358720 | bytes 11534336 | tf_op jit(solution)/shard_map/dot_general | solution.py:77
  379.3 7.1 %multiply_convert_fusion = bf16[3584,512]{1,0:T(8,128)(2,1)} fusion(bf16[768,3584]{1,0:T(8,128)(2,1)} %bitcast.55, bf16[768,512]{1,0:T(8,128)(2,1)S(1)} %all_gather.13), kind=kOutput, calls=%fused_computation.7 | convolution fusion | flops 2822242304 | bytes 9961472 | tf_op jit(solution)/shard_map/dot_general | solution.py:65
  386.4 7.2 %fusion.4 = bf16[512,3584]{0,1:T(8,128)(2,1)} fusion(bf16[768,3584]{1,0:T(8,128)(2,1)} %all-gather.3.cloned.1.call-done, bf16[768,512]{1,0:T(8,128)(2,1)S(1)} %all_gather.12), kind=kOutput, calls=%fused_computation.11 | convolution fusion | flops 2822242304 | bytes 9961472 | tf_op jit(solution)/shard_map/dot_general | solution.py:68
  393.6 5.9 %copy.26 = bf16[512,3584]{1,0:T(8,128)(2,1)} copy(bf16[512,3584]{0,1:T(8,128)(2,1)} %fusion.4) | data formatting | bytes 7340032
  399.5 7.2 %fusion.5 = bf16[512,3584]{0,1:T(8,128)(2,1)} fusion(bf16[768,3584]{1,0:T(8,128)(2,1)} %all-gather.5.cloned.1.call-done, bf16[768,512]{1,0:T(8,128)(2,1)S(1)} %all_gather.12), kind=kOutput, calls=%fused_computation.12 | convolution fusion | flops 2822242304 | bytes 9961472 | tf_op jit(solution)/shard_map/dot_general | solution.py:71
  406.7 5.9 %copy.27 = bf16[512,3584]{1,0:T(8,128)(2,1)} copy(bf16[512,3584]{0,1:T(8,128)(2,1)} %fusion.5) | data formatting | bytes 7340032
  (60 shorter events, 29.9 us)
Async XLA Ops:
  7.2 201.4 %reduce-scatter.7.cloned.1.call-start = ((), (), s32[]{:S(2)}) async-start(), calls=%async_computation.5 | async-start | bytes 17547264 | tf_op jit(solution)/shard_map/reduce_scatter | solution.py:41
  97.8 251.8 %all-gather.3.cloned.1.call-start = ((), (), s32[]{:S(2)}) async-start(), calls=%async_computation.2 | async-start | bytes 5849088 | tf_op jit(solution)/shard_map/all_gather | solution.py:61
  211.1 160.5 %all-gather.5.cloned.1.call-start = ((), (), s32[]{:S(2)}) async-start(), calls=%async_computation.3 | async-start | bytes 5849088 | tf_op jit(solution)/shard_map/all_gather | solution.py:62
  211.2 12.8 %collective-permute-start = (bf16[48,3584]{1,0:T(8,128)(2,1)S(1)}, bf16[48,3584]{1,0:T(8,128)(2,1)S(1)}, u32[]{:S(2)}, u32[]{:S(2)}) collective-permute-start(bf16[48,3584]{1,0:T(8,128)(2,1)S(1)} %get-tuple-element.20), channel_id=1, source_target_pairs={{0,8},{8,16},{16,24},{24,32},{32,40},{40,48},{48,56},{56,64},{64,7... | collective-permute-start | bytes 1032200 | tf_op jit(solution)/shard_map/ppermute | solution.py:54
  224.0 16.0 %collective-permute-start.1 = (bf16[48,3584]{1,0:T(8,128)(2,1)S(1)}, bf16[48,3584]{1,0:T(8,128)(2,1)S(1)}, u32[]{:S(2)}, u32[]{:S(2)}) collective-permute-start(bf16[48,3584]{1,0:T(8,128)(2,1)S(1)} %collective-permute-done), channel_id=1, source_target_pairs={{0,8},{8,16},{16,24},{24,32},{32,40},{40,48},{48,56},{56,64},{64,7... | collective-permute-start | bytes 1032200 | tf_op jit(solution)/shard_map/ppermute | solution.py:54
  224.0 16.0 %collective-permute-start.8 = (bf16[48,3584]{1,0:T(8,128)(2,1)S(1)}, bf16[48,3584]{1,0:T(8,128)(2,1)S(1)}, u32[]{:S(2)}, u32[]{:S(2)}) collective-permute-start(bf16[48,3584]{1,0:T(8,128)(2,1)S(1)} %get-tuple-element.20), channel_id=1, source_target_pairs={{8,0},{16,8},{24,16},{32,24},{40,32},{48,40},{56,48},{64,56},{72,6... | collective-permute-start | bytes 1032200 | tf_op jit(solution)/shard_map/ppermute | solution.py:56
  240.0 12.0 %collective-permute-start.2 = (bf16[48,3584]{1,0:T(8,128)(2,1)S(1)}, bf16[48,3584]{1,0:T(8,128)(2,1)S(1)}, u32[]{:S(2)}, u32[]{:S(2)}) collective-permute-start(bf16[48,3584]{1,0:T(8,128)(2,1)S(1)} %collective-permute-done.1), channel_id=1, source_target_pairs={{0,8},{8,16},{16,24},{24,32},{32,40},{40,48},{48,56},{56,64},{64,7... | collective-permute-start | bytes 1032200 | tf_op jit(solution)/shard_map/ppermute | solution.py:54
  240.0 18.1 %collective-permute-start.9 = (bf16[48,3584]{1,0:T(8,128)(2,1)S(1)}, bf16[48,3584]{1,0:T(8,128)(2,1)S(1)}, u32[]{:S(2)}, u32[]{:S(2)}) collective-permute-start(bf16[48,3584]{1,0:T(8,128)(2,1)S(1)} %collective-permute-done.8), channel_id=1, source_target_pairs={{8,0},{16,8},{24,16},{32,24},{40,32},{48,40},{56,48},{64,56},{72,6... | collective-permute-start | bytes 1032200 | tf_op jit(solution)/shard_map/ppermute | solution.py:56
  252.0 25.5 %copy-start = (bf16[48,3584]{1,0:T(8,128)(2,1)}, bf16[48,3584]{1,0:T(8,128)(2,1)S(1)}, u32[]{:S(2)}) copy-start(bf16[48,3584]{1,0:T(8,128)(2,1)S(1)} %collective-permute-done.2) | copy-start | bytes 1032196
  252.0 20.5 %collective-permute-start.3 = (bf16[48,3584]{1,0:T(8,128)(2,1)S(1)}, bf16[48,3584]{1,0:T(8,128)(2,1)S(1)}, u32[]{:S(2)}, u32[]{:S(2)}) collective-permute-start(bf16[48,3584]{1,0:T(8,128)(2,1)S(1)} %collective-permute-done.2), channel_id=1, source_target_pairs={{0,8},{8,16},{16,24},{24,32},{32,40},{40,48},{48,56},{56,64},{64,7... | collective-permute-start | bytes 1032200 | tf_op jit(solution)/shard_map/ppermute | solution.py:54
  258.1 19.3 %collective-permute-start.10 = (bf16[48,3584]{1,0:T(8,128)(2,1)S(1)}, bf16[48,3584]{1,0:T(8,128)(2,1)S(1)}, u32[]{:S(2)}, u32[]{:S(2)}) collective-permute-start(bf16[48,3584]{1,0:T(8,128)(2,1)S(1)} %collective-permute-done.9), channel_id=1, source_target_pairs={{8,0},{16,8},{24,16},{32,24},{40,32},{48,40},{56,48},{64,56},{72,6... | collective-permute-start | bytes 1032200 | tf_op jit(solution)/shard_map/ppermute | solution.py:56
  272.4 29.4 %copy-start.5 = (bf16[48,3584]{1,0:T(8,128)(2,1)}, bf16[48,3584]{1,0:T(8,128)(2,1)S(1)}, u32[]{:S(2)}) copy-start(bf16[48,3584]{1,0:T(8,128)(2,1)S(1)} %collective-permute-done.3) | copy-start | bytes 1032196
  272.4 17.6 %collective-permute-start.4 = (bf16[48,3584]{1,0:T(8,128)(2,1)S(1)}, bf16[48,3584]{1,0:T(8,128)(2,1)S(1)}, u32[]{:S(2)}, u32[]{:S(2)}) collective-permute-start(bf16[48,3584]{1,0:T(8,128)(2,1)S(1)} %collective-permute-done.3), channel_id=1, source_target_pairs={{0,8},{8,16},{16,24},{24,32},{32,40},{40,48},{48,56},{56,64},{64,7... | collective-permute-start | bytes 1032200 | tf_op jit(solution)/shard_map/ppermute | solution.py:54
  277.5 5.8 %copy-start.1 = (bf16[48,3584]{1,0:T(8,128)(2,1)}, bf16[48,3584]{1,0:T(8,128)(2,1)S(1)}, u32[]{:S(2)}) copy-start(bf16[48,3584]{1,0:T(8,128)(2,1)S(1)} %collective-permute-done.10) | copy-start | bytes 1032196
  277.5 12.5 %collective-permute-start.11 = (bf16[48,3584]{1,0:T(8,128)(2,1)S(1)}, bf16[48,3584]{1,0:T(8,128)(2,1)S(1)}, u32[]{:S(2)}, u32[]{:S(2)}) collective-permute-start(bf16[48,3584]{1,0:T(8,128)(2,1)S(1)} %collective-permute-done.10), channel_id=1, source_target_pairs={{8,0},{16,8},{24,16},{32,24},{40,32},{48,40},{56,48},{64,56},{72,6... | collective-permute-start | bytes 1032200 | tf_op jit(solution)/shard_map/ppermute | solution.py:56
  290.0 17.7 %copy-start.6 = (bf16[48,3584]{1,0:T(8,128)(2,1)}, bf16[48,3584]{1,0:T(8,128)(2,1)S(1)}, u32[]{:S(2)}) copy-start(bf16[48,3584]{1,0:T(8,128)(2,1)S(1)} %collective-permute-done.4) | copy-start | bytes 1032196
  290.0 11.8 %collective-permute-start.5 = (bf16[48,3584]{1,0:T(8,128)(2,1)S(1)}, bf16[48,3584]{1,0:T(8,128)(2,1)S(1)}, u32[]{:S(2)}, u32[]{:S(2)}) collective-permute-start(bf16[48,3584]{1,0:T(8,128)(2,1)S(1)} %collective-permute-done.4), channel_id=1, source_target_pairs={{0,8},{8,16},{16,24},{24,32},{32,40},{40,48},{48,56},{56,64},{64,7... | collective-permute-start | bytes 1032200 | tf_op jit(solution)/shard_map/ppermute | solution.py:54
  290.0 0.8 copy-start.3
  290.8 11.0 %collective-permute-start.12 = (bf16[48,3584]{1,0:T(8,128)(2,1)S(1)}, bf16[48,3584]{1,0:T(8,128)(2,1)}, u32[]{:S(2)}, u32[]{:S(2)}) collective-permute-start(bf16[48,3584]{1,0:T(8,128)(2,1)S(1)} %collective-permute-done.11), channel_id=1, source_target_pairs={{8,0},{16,8},{24,16},{32,24},{40,32},{48,40},{56,48},{64,56},{72,6... | collective-permute-start | bytes 1032200 | tf_op jit(solution)/shard_map/ppermute | solution.py:56
  301.8 10.9 %copy-start.7 = (bf16[48,3584]{1,0:T(8,128)(2,1)}, bf16[48,3584]{1,0:T(8,128)(2,1)S(1)}, u32[]{:S(2)}) copy-start(bf16[48,3584]{1,0:T(8,128)(2,1)S(1)} %collective-permute-done.5) | copy-start | bytes 1032196
  301.8 10.9 %collective-permute-start.6 = (bf16[48,3584]{1,0:T(8,128)(2,1)S(1)}, bf16[48,3584]{1,0:T(8,128)(2,1)}, u32[]{:S(2)}, u32[]{:S(2)}) collective-permute-start(bf16[48,3584]{1,0:T(8,128)(2,1)S(1)} %collective-permute-done.5), channel_id=1, source_target_pairs={{0,8},{8,16},{16,24},{24,32},{32,40},{40,48},{48,56},{56,64},{64,7... | collective-permute-start | bytes 1032200 | tf_op jit(solution)/shard_map/ppermute | solution.py:54
  301.8 11.0 %collective-permute-start.13 = (bf16[48,3584]{1,0:T(8,128)(2,1)}, bf16[48,3584]{1,0:T(8,128)(2,1)}, u32[]{:S(2)}, u32[]{:S(2)}) collective-permute-start(bf16[48,3584]{1,0:T(8,128)(2,1)} %collective-permute-done.12), channel_id=1, source_target_pairs={{8,0},{16,8},{24,16},{32,24},{40,32},{48,40},{56,48},{64,56},{72,6... | collective-permute-start | bytes 1032200 | tf_op jit(solution)/shard_map/ppermute | solution.py:56
  312.7 10.9 %collective-permute-start.7 = (bf16[48,3584]{1,0:T(8,128)(2,1)}, bf16[48,3584]{1,0:T(8,128)(2,1)}, u32[]{:S(2)}, u32[]{:S(2)}) collective-permute-start(bf16[48,3584]{1,0:T(8,128)(2,1)} %collective-permute-done.6), channel_id=1, source_target_pairs={{0,8},{8,16},{16,24},{24,32},{32,40},{40,48},{48,56},{56,64},{64,7... | collective-permute-start | bytes 1032200 | tf_op jit(solution)/shard_map/ppermute | solution.py:54
  312.8 99.9 %reduce-scatter.5.cloned.1.call-start = ((), (), s32[]{:S(2)}) async-start(), calls=%async_computation.4 | async-start | bytes 884736 | tf_op jit(solution)/shard_map/reduce_scatter | solution.py:84
  312.8 25.1 %copy-start.2 = (bf16[48,3584]{1,0:T(8,128)(2,1)S(1)}, bf16[48,3584]{1,0:T(8,128)(2,1)}, u32[]{:S(2)}) copy-start(bf16[48,3584]{1,0:T(8,128)(2,1)} %copy-done.1) | copy-start | bytes 1032196
  312.8 25.8 %copy-start.4 = (bf16[48,3584]{1,0:T(8,128)(2,1)S(1)}, bf16[48,3584]{1,0:T(8,128)(2,1)}, u32[]{:S(2)}) copy-start(bf16[48,3584]{1,0:T(8,128)(2,1)} %copy-done.3) | copy-start | bytes 1032196
  312.9 30.1 %collective-permute-start.14 = (bf16[48,3584]{1,0:T(8,128)(2,1)}, bf16[48,3584]{1,0:T(8,128)(2,1)S(1)}, u32[]{:S(2)}, u32[]{:S(2)}) collective-permute-start(bf16[48,3584]{1,0:T(8,128)(2,1)} %collective-permute-done.13), channel_id=1, source_target_pairs={{8,0},{16,8},{24,16},{32,24},{40,32},{48,40},{56,48},{64,56},{72,6... | collective-permute-start | bytes 1032200 | tf_op jit(solution)/shard_map/ppermute | solution.py:56
Sparse Core Ops, SparseCore 0:
  97.9 110.5 reduce-scatter.6
  211.5 77.0 all-gather.2
  312.9 58.7 all-gather.4
  379.4 31.2 reduce-scatter.4
